TPU v7x, 32 devices: a whole 2x2x4 slice. The times are simulated.
32 devices in a mesh: blk: 8 (over z, y), grp: 4 (over x, core).
Axes of the slice: x: 2, y: 2, z: 4, core: 2. Of those that a mesh axis runs over, the one named last changes fastest.
Arguments:
- embeddings: bfloat16 [4, 4096, 1024], P('grp', 'blk'), may hold values from -12 to 12
- strata: int32 [4, 4096], P('grp', 'blk'), may hold values from 0 to 127, as said below
- centroids: bfloat16 [4, 128, 1024], P('grp', 'blk'), may hold values from -12 to 12
Outputs:
- probs: float32 [4, 4096], P('grp', 'blk')
Inputs may be any that keep to these rules, and one draw needn't show every extreme that they name: `strata`: within each aligned run of 512 rows of a collection the stratum ids never fall; within each range of 16 consecutive ids the smallest are about four times as common as the largest. `strata`: in each aligned run of 512 rows, at most 128 rows have ids in one range k * 16 to (k + 1) * 16 - 1, and exactly 128 in some range.
All inputs are finite; a program needn't handle non-finite values.
Results may differ from a plain program's by a relative error of at most 0.0014.
Values may be sent and summed in bfloat16 or wider, within the bound.
No kernel may reach another device: no remote copies, remote signals or barrier semaphores. Data moves between devices by JAX's collectives and lax.ppermute only.
A program may use at most 64 MiB of HBM per device.

v0:
```python
import math
import jax
import jax.numpy as jnp
from jax import lax
from jax.sharding import PartitionSpec as P

sharpness_divisor = 0.25
base_term = 0.05
epsilon = 1e-06


def unit_rows(matrix):
    values = matrix.astype(jnp.float32)
    scaling = lax.rsqrt(jnp.mean(values * values, axis=-1, keepdims=True) + epsilon) / math.sqrt(
        matrix.shape[-1]
    )
    return (values * scaling).astype(jnp.bfloat16)


def dense_sums(query_rows, query_ids, key_rows, key_ids):
    logit_entries = lax.dot_general(
        query_rows, key_rows, (((1,), (1,)), ((), ())), preferred_element_type=jnp.float32
    )
    similarity_grid = jnp.where(
        query_ids[:, None] == key_ids[None, :],
        jnp.exp((logit_entries - 1.0) / sharpness_divisor),
        jnp.zeros_like(logit_entries),
    )
    return (jnp.sum(similarity_grid, axis=1), jnp.sum(similarity_grid, axis=0))


def pair_sums(query_rows, query_ids, key_rows, key_ids):
    return dense_sums(query_rows, query_ids, key_rows, key_ids)


def body(embeddings, strata, centroids):
    own_units = unit_rows(embeddings[0])
    own_ids = strata[0]
    row_count = own_units.shape[0]
    cent_local = unit_rows(centroids[0])
    cent_units = lax.all_gather(cent_local, "blk", axis=0, tiled=True)
    strata_count = cent_units.shape[0]
    selector = (own_ids[:, None] == lax.broadcasted_iota(jnp.int32, (1, strata_count), 1)).astype(
        jnp.bfloat16
    )
    picked = jnp.dot(selector, cent_units, preferred_element_type=jnp.float32)
    distance = 1.0 - jnp.sum(own_units.astype(jnp.float32) * picked, axis=-1)
    guest_rows = lax.all_gather(own_units, "blk", axis=0, tiled=True)
    guest_ids = lax.all_gather(own_ids, "blk", axis=0, tiled=True)
    row_sums, column_sums = pair_sums(own_units, own_ids, guest_rows, guest_ids)
    weights = (distance + base_term) / row_sums
    total = lax.psum(jnp.sum(weights), ("blk", "grp"))
    row_total = float(row_count * lax.axis_size("blk") * lax.axis_size("grp"))
    return (weights * (row_total / total))[None, :]


def solution(mesh):
    placed = (P("grp", "blk", None), P("grp", "blk"), P("grp", "blk", None))
    return jax.shard_map(
        body, mesh=mesh, in_specs=placed, out_specs=P("grp", "blk"), check_vma=False
    )
```

profile of v0, /device:TPU:0, one launch (start us, length us, event | category | flops | bytes accessed | tf_op | source)
XLA Modules:
  0.0 197.1 jit_solution(4007569216989032687)
XLA Ops:
  6.5 0.0 all-gather.3.cloned.1.call-start
  6.5 1.5 fusion
  8.1 2.5 %fusion.1 = bf16[512,1024]{1,0:T(8,128)(2,1)} fusion(bf16[1,512,1024]{2,1,0:T(8,128)(2,1)} %param.3, f32[512]{0:T(512)S(1)} %rsqrt_multiply_fusion), kind=kLoop, calls=%fused_computation.4 | loop fusion | flops 1572864 | bytes 2099200 | tf_op jit(solution)/shard_map/convert_element_type | solution.py:17
  10.6 0.0 all-gather.3.cloned.1.call-update
  10.6 28.4 %all-gather = s32[1,4096]{1,0:T(1,128)S(1)} all-gather(s32[1,512]{1,0:T(1,128)} %param.4), channel_id=2, replica_groups=mesh['blk'=8,'grp'=4] {'blk'}, dimensions={1}, use_global_device_ids=true | all-gather | bytes 18432 | tf_op jit(solution)/shard_map/all_gather | solution.py:49
  39.0 0.9 fusion.3
  39.9 0.8 fusion.4
  40.7 31.6 %all_gather.9 = bf16[128,1024]{1,0:T(8,128)(2,1)S(1)} all-gather(bf16[16,1024]{1,0:T(8,128)(2,1)S(1)} %fusion.4), channel_id=1, replica_groups=mesh['blk'=8,'grp'=4] {'blk'}, dimensions={0}, use_global_device_ids=true | all-gather | bytes 294912 | tf_op jit(solution)/shard_map/all_gather | solution.py:41
  72.3 1.8 multiply_reduce_fusion
  74.1 66.4 %all-gather.3.cloned.1.call-done = bf16[4096,1024]{1,0:T(8,128)(2,1)} async-done(((bf16[512,1024]{1,0:T(8,128)(2,1)}), bf16[4096,1024]{1,0:T(8,128)(2,1)}) %all-gather.3.cloned.1.call-update) | async-done | bytes 8388624 | tf_op jit(solution)/shard_map/all_gather | solution.py:48
  140.5 9.1 %select_reduce_fusion = f32[512]{0:T(512)S(1)} fusion(bf16[512,1024]{1,0:T(8,128)(2,1)} %fusion.1, bf16[4096,1024]{1,0:T(8,128)(2,1)} %all-gather.3.cloned.1.call-done, s32[4096]{0:T(1024)S(1)} %bitcast.14, s32[512]{0:T(512)} %bitcast.16), kind=kOutput, calls=%fused_computation | convolution fusion | flops 4305452544 | bytes 9457664 | tf_op jit(solution)/shard_map/dot_general | solution.py:21
  149.6 0.6 fusion.5
  150.2 38.8 %psum.7 = f32[]{:T(128)} all-reduce(f32[]{:T(128)} %get-tuple-element.5), channel_id=1, replica_groups=mesh['blk'=8,'grp'=4] {'blk','grp'}, use_global_device_ids=true, to_apply=%region_5.6 | all-reduce | flops 1 | bytes 8 | tf_op jit(solution)/shard_map/psum | solution.py:52
  189.7 0.6 broadcast_multiply_fusion
  (2 shorter events, 0.0 us)
Async XLA Ops:
  6.5 134.0 %all-gather.3.cloned.1.call-start = ((), (), s32[]{:S(2)}) async-start(), calls=%async_computation | async-start | bytes 9437184 | tf_op jit(solution)/shard_map/all_gather | solution.py:48
Sparse Core Ops, SparseCore 0:
  10.7 129.7 all-gather.2
where the time goes:
time: 198 us; the launch traced here: 197 us
  blocking collectives  98.8 us (50%)
  waiting for transfers between devices  66.4 us (34%)
  between operations  14.1 us (7%)
  matrix products  10.9 us (6%)
  other arithmetic  6.97 us (4%)
    all_gather x1, waiting for transfers between devices, body(): guest_rows = lax.all_gather(own_units, 'blk', axis=0, tiled=True)  66.4 us
    psum x1, blocking collectives, body(): total = lax.psum(jnp.sum(weights), ('blk', 'grp'))  38.8 us
    all_gather x1, blocking collectives, body(): cent_units = lax.all_gather(cent_local, 'blk', axis=0, tiled=True)  31.6 us
    all_gather x1, blocking collectives, body(): guest_ids = lax.all_gather(own_ids, 'blk', axis=0, tiled=True)  28.4 us
    dot_general x1, matrix products, dense_sums(): lax.dot_general(query_rows, key_rows, (((1,), (1,)), ((), ())), preferred...  9.08 us
  transfers between devices with their start and end apart: 1, of which 1 were waited for; matrix products, arithmetic and copies ran while one was open for 2% of the time, Pallas kernels for 0%

commit v1 on v0

--- a/solution.py
+++ b/solution.py
@@ -46,7 +46,10 @@
     picked = jnp.dot(selector, cent_units, preferred_element_type=jnp.float32)
     distance = 1.0 - jnp.sum(own_units.astype(jnp.float32) * picked, axis=-1)
     guest_rows = lax.all_gather(own_units, "blk", axis=0, tiled=True)
-    guest_ids = lax.all_gather(own_ids, "blk", axis=0, tiled=True)
+    size = lax.axis_size("blk")
+    blocks = jnp.stack([own_ids for _ in range(size)])
+    blocks = lax.all_to_all(blocks, "blk", split_axis=0, concat_axis=0)
+    guest_ids = jnp.concatenate(blocks, axis=0)
     row_sums, column_sums = pair_sums(own_units, own_ids, guest_rows, guest_ids)
     weights = (distance + base_term) / row_sums
     total = lax.psum(jnp.sum(weights), ("blk", "grp"))

time: 198 us -> 198 us (level)
  blocking collectives: 98.8 us -> 71.3 us
  waiting for transfers between devices: 66.4 us -> 85.2 us
  starting transfers between devices: 0.01 us -> 7.28 us
    all_gather x1 -> x0, blocking collectives: 28.4 us -> none  [body(): guest_ids = lax.all_gather(own_ids, 'blk', axis=0, tiled=True)]
    all_gather x1, waiting for transfers between devices: 66.4 us -> 85.2 us  [body(): guest_rows = lax.all_gather(own_units, 'blk', axis=0, tiled=True)]
    all_to_all x0 -> x1, starting transfers between devices: none -> 7.28 us  [body(): blocks = lax.all_to_all(blocks, 'blk', split_axis=0, concat_axis=0)]
  transfers between devices with their start and end apart: 1 -> 2, of which waited for: 1 -> 1; matrix products, arithmetic and copies ran while one was open for 2% -> 2% of each run, Pallas kernels for 0% -> 0%
where the time goes in v1:
time: 198 us; the launch traced here: 197 us
  waiting for transfers between devices  85.2 us (43%)
  blocking collectives  71.3 us (36%)
  between operations  14.1 us (7%)
  matrix products  10.9 us (6%)
  starting transfers between devices  7.28 us (4%)
  other arithmetic  6.98 us (4%)
    all_gather x1, waiting for transfers between devices, body(): guest_rows = lax.all_gather(own_units, 'blk', axis=0, tiled=True)  85.2 us
    psum x1, blocking collectives, body(): total = lax.psum(jnp.sum(weights), ('blk', 'grp'))  38.6 us
    all_gather x1, blocking collectives, body(): cent_units = lax.all_gather(cent_local, 'blk', axis=0, tiled=True)  32.7 us
    dot_general x1, matrix products, dense_sums(): lax.dot_general(query_rows, key_rows, (((1,), (1,)), ((), ())), preferred...  9.08 us
    all_to_all x1, starting transfers between devices, body(): blocks = lax.all_to_all(blocks, 'blk', split_axis=0, concat_axis=0)  7.28 us
  transfers between devices with their start and end apart: 2, of which 1 were waited for; matrix products, arithmetic and copies ran while one was open for 2% of the time, Pallas kernels for 0%

profile of v1, /device:TPU:0, one launch (start us, length us, event | category | flops | bytes accessed | tf_op | source)
XLA Modules:
  0.0 197.1 jit_solution(4731645907116196583)
XLA Ops:
  6.5 0.0 all-gather.2.cloned.1.call-start
  6.5 1.5 fusion
  8.1 2.5 %fusion.1 = bf16[512,1024]{1,0:T(8,128)(2,1)} fusion(bf16[1,512,1024]{2,1,0:T(8,128)(2,1)} %param.3, f32[512]{0:T(512)S(1)} %rsqrt_multiply_fusion), kind=kLoop, calls=%fused_computation.4 | loop fusion | flops 1572864 | bytes 2099200 | tf_op jit(solution)/shard_map/convert_element_type | solution.py:17
  10.6 0.0 all-gather.2.cloned.1.call-update
  10.6 1.3 stack.3
  11.9 7.3 %all-to-all-start = ((s32[8,1,512]{2,1,0:T(1,128)}), s32[8,1,512]{2,1,0:T(1,128)S(1)}, u32[]{:S(2)}, u32[]{:S(2)}) async-start(s32[8,1,512]{2,1,0:T(1,128)} %stack.3), calls=%async_computation | async-start | bytes 32768 | tf_op jit(solution)/shard_map/all_to_all | solution.py:51
  19.2 0.9 fusion.3
  20.1 0.8 fusion.4
  20.9 32.7 %all_gather.6 = bf16[128,1024]{1,0:T(8,128)(2,1)S(1)} all-gather(bf16[16,1024]{1,0:T(8,128)(2,1)S(1)} %fusion.4), channel_id=1, replica_groups=mesh['blk'=8,'grp'=4] {'blk'}, dimensions={0}, use_global_device_ids=true | all-gather | bytes 294912 | tf_op jit(solution)/shard_map/all_gather | solution.py:41
  53.7 1.8 multiply_reduce_fusion
  55.5 0.0 all-to-all-done
  55.5 85.2 %all-gather.2.cloned.1.call-done = bf16[4096,1024]{1,0:T(8,128)(2,1)} async-done(((bf16[512,1024]{1,0:T(8,128)(2,1)}), bf16[4096,1024]{1,0:T(8,128)(2,1)}) %all-gather.2.cloned.1.call-update) | async-done | bytes 8388624 | tf_op jit(solution)/shard_map/all_gather | solution.py:48
  140.6 9.1 %select_reduce_fusion = f32[512]{0:T(512)S(1)} fusion(bf16[512,1024]{1,0:T(8,128)(2,1)} %fusion.1, bf16[4096,1024]{1,0:T(8,128)(2,1)} %all-gather.2.cloned.1.call-done, s32[4096]{0:T(1024)S(1)} %bitcast.14, s32[512]{0:T(512)} %bitcast.17), kind=kOutput, calls=%fused_computation | convolution fusion | flops 4305452544 | bytes 9457664 | tf_op jit(solution)/shard_map/dot_general | solution.py:21
  149.7 0.6 fusion.5
  150.3 38.6 %psum.7 = f32[]{:T(128)} all-reduce(f32[]{:T(128)} %get-tuple-element.5), channel_id=1, replica_groups=mesh['blk'=8,'grp'=4] {'blk','grp'}, use_global_device_ids=true, to_apply=%region_5.6 | all-reduce | flops 1 | bytes 8 | tf_op jit(solution)/shard_map/psum | solution.py:55
  189.6 0.6 broadcast_multiply_fusion
  (2 shorter events, 0.0 us)
Async XLA Ops:
  6.5 134.1 %all-gather.2.cloned.1.call-start = ((), (), s32[]{:S(2)}) async-start(), calls=%async_computation.1 | async-start | bytes 9437184 | tf_op jit(solution)/shard_map/all_gather | solution.py:48
  11.9 43.6 %all-to-all-start = ((s32[8,1,512]{2,1,0:T(1,128)}), s32[8,1,512]{2,1,0:T(1,128)S(1)}, u32[]{:S(2)}, u32[]{:S(2)}) async-start(s32[8,1,512]{2,1,0:T(1,128)} %stack.3), calls=%async_computation | async-start | bytes 32768 | tf_op jit(solution)/shard_map/all_to_all | solution.py:51
Sparse Core Ops, SparseCore 0:
  10.7 129.8 all-gather.1
